TPU v7x, 32 devices: a whole 2x2x4 slice. The times are simulated.
32 devices in a mesh: fsdp: 16 (over z, y, x), tp: 2 (over core).
Axes of the slice: x: 2, y: 2, z: 4, core: 2. Of those that a mesh axis runs over, the one named last changes fastest.
Arguments:
- owner: int32 [2, 7], replicated, may hold values from 0 to 15, as said below
- grads: bfloat16 [2, 896, 2, 8320], P(None, 'fsdp', 'tp')
- weights: float32 [2, 896, 2, 8320], P(None, 'fsdp', 'tp'), may hold values from -0.1875 to 0.1875
- adam_m: float32 [2, 896, 2, 8320], P(None, 'fsdp', 'tp'), may hold values from -0.4375 to 0.4375
- adam_v: float32 [2, 896, 2, 8320], P(None, 'fsdp', 'tp'), may hold values from 0.0001 to 0.1
- stats: float32 [16, 896, 896], P('fsdp', 'tp')
- roots: bfloat16 [16, 896, 896], P('fsdp', 'tp')
- vec_weight: float32 [2, 2944], P(None, ('fsdp', 'tp')), may hold values from 0.5 to 1.5
- vec_grad: bfloat16 [2, 2944], P(None, ('fsdp', 'tp')), may hold values from -1.5 to 1.5
- vec_m: float32 [2, 2944], P(None, ('fsdp', 'tp')), may hold values from -0.4375 to 0.4375
- vec_v: float32 [2, 2944], P(None, ('fsdp', 'tp')), may hold values from 0.0001 to 0.1
Outputs:
- weights_new: float32 [2, 896, 2, 8320], P(None, 'fsdp', 'tp')
- adam_m_new: float32 [2, 896, 2, 8320], P(None, 'fsdp', 'tp')
- adam_v_new: float32 [2, 896, 2, 8320], P(None, 'fsdp', 'tp')
- stats_new: float32 [16, 896, 896], P('fsdp', 'tp')
- vec_weight_new: float32 [2, 2944], P(None, ('fsdp', 'tp'))
- vec_m_new: float32 [2, 2944], P(None, ('fsdp', 'tp'))
- vec_v_new: float32 [2, 2944], P(None, ('fsdp', 'tp'))
Inputs may be any that keep to these rules, and one draw needn't show every extreme that they name: owner[l, t] is the index along fsdp of the chip whose slot holds the statistic of kind t of layer l; all 14 values are distinct, so a chip owns at most one matrix and some chips own none.
All inputs are finite; a program needn't handle non-finite values.
Results may differ from a plain program's by a relative error of at most 0.0015.
Values may be sent and summed in bfloat16 or wider, within the bound.
No kernel may reach another device: no remote copies, remote signals or barrier semaphores. Data moves between devices by JAX's collectives and lax.ppermute only.
A program may use at most 192 MiB of HBM per device.

v0:
```python
import jax
import jax.numpy as jnp
from jax import lax
from jax.sharding import PartitionSpec as P

FF = 4864
QW = 896
KW = 128


def half_widths():
    return [QW // 2, KW // 2, KW // 2, QW // 2, FF // 2, FF // 2, FF // 2]


def column_starts(widths):
    starts = []
    position = 0
    for wide in widths:
        starts.append(position)
        position = position + wide
    return starts


def kind_sums(values, widths, starts):
    return jnp.stack(
        [
            jnp.sum(values[:, :, starts[kind] : starts[kind] + widths[kind]], axis=(1, 2))
            for kind in range(7)
        ],
        axis=1,
    )


def gram_rows(left, right):
    return lax.dot_general(
        left, right, (((1,), (1,)), ((), ())), preferred_element_type=jnp.float32
    )


def on_device(
    owner, grads, weights, adam_m, adam_v, stats, roots, vec_weight, vec_grad, vec_m, vec_v
):
    widths = half_widths()
    starts = column_starts(widths)
    classes = [widths[0], widths[1], widths[4]]
    class_table = jnp.array([0, 1, 1, 0, 2, 2, 2], jnp.int32)
    chips = lax.axis_size("fsdp")
    layers = grads.shape[0]
    rows = grads.shape[1]
    capacity = FF // 2
    model_rows = rows * chips
    local_grad = grads[:, :, 0, :]
    grad_float = grads.astype(jnp.float32)
    adam_m_new = 0.9 * adam_m + 0.1 * grad_float
    adam_v_new = 0.99 * adam_v + 0.01 * grad_float * grad_float
    adam_step = (adam_m_new / (jnp.sqrt(adam_v_new) + 1e-08))[:, :, 0, :]
    adam_part = kind_sums(adam_step * adam_step, widths, starts)
    adam_total = lax.psum(adam_part, ("fsdp", "tp"))
    outgoing = jnp.zeros((chips, rows, capacity), jnp.bfloat16)
    for kind in range(7):
        outgoing = outgoing.at[owner[:, kind], :, : widths[kind]].set(
            local_grad[:, :, starts[kind] : starts[kind] + widths[kind]]
        )
    arrived = lax.all_to_all(outgoing, "fsdp", split_axis=0, concat_axis=0, tiled=True)
    gathered = arrived.reshape(model_rows, capacity)
    chip_index = lax.axis_index("fsdp")
    matches = owner == chip_index
    owned = jnp.any(matches)
    width_class = jnp.where(owned, jnp.sum(jnp.where(matches, class_table[None, :], 0)), 1)
    stat_slot = stats[0]
    root_slot = roots[0]

    def stat_term_rows():

        def make_rows(wide):

            def branch():
                block = gathered[:, :wide]
                return gram_rows(block, gathered[:, :wide])

            return branch

        return lax.switch(width_class, [make_rows(wide) for wide in classes])

    stat_term = lax.psum_scatter(stat_term_rows(), "tp", scatter_dimension=0, tiled=True)

    def apply_rows(piece):

        def make_apply(wide):

            def branch():
                result = jnp.dot(piece, gathered[:, :wide], preferred_element_type=jnp.float32)
                return jnp.pad(result, ((0, 0), (0, capacity - wide)))

            return branch

        return lax.switch(width_class, [make_apply(wide) for wide in classes])

    precond = apply_rows(lax.all_gather(root_slot, "tp", axis=0, tiled=True)).astype(jnp.bfloat16)
    stats_new = jnp.where(owned, 0.9 * stat_slot + 0.1 * stat_term, stat_slot)[None]
    returned = lax.all_to_all(
        precond.reshape(chips, rows, capacity), "fsdp", split_axis=0, concat_axis=0, tiled=True
    )
    pieces = [returned[owner[:, kind], :, : widths[kind]] for kind in range(7)]
    direction = jnp.concatenate(pieces, axis=2).astype(jnp.float32)
    shampoo_part = kind_sums(direction * direction, widths, starts)
    shampoo_total = lax.psum(shampoo_part, ("fsdp", "tp"))
    ratio = jnp.sqrt(adam_total) / (jnp.sqrt(shampoo_total) + 1e-06)
    column_scale = jnp.concatenate(
        [jnp.broadcast_to(ratio[:, kind : kind + 1], (layers, widths[kind])) for kind in range(7)],
        axis=1,
    )
    weights_new = weights - 0.02 * (direction * column_scale[:, None, :])[:, :, None, :]
    vec_float = vec_grad.astype(jnp.float32)
    vec_m_new = 0.9 * vec_m + 0.1 * vec_float
    vec_v_new = 0.99 * vec_v + 0.01 * vec_float * vec_float
    vec_weight_new = vec_weight - 0.02 * vec_m_new / (jnp.sqrt(vec_v_new) + 1e-08)
    return (weights_new, adam_m_new, adam_v_new, stats_new, vec_weight_new, vec_m_new, vec_v_new)


def solution(mesh):
    placed = (
        P(),
        P(None, "fsdp", "tp", None),
        P(None, "fsdp", "tp", None),
        P(None, "fsdp", "tp", None),
        P(None, "fsdp", "tp", None),
        P("fsdp", "tp", None),
        P("fsdp", "tp", None),
        P(None, ("fsdp", "tp")),
        P(None, ("fsdp", "tp")),
        P(None, ("fsdp", "tp")),
        P(None, ("fsdp", "tp")),
    )
    return jax.shard_map(
        on_device,
        mesh=mesh,
        in_specs=placed,
        out_specs=(
            P(None, "fsdp", "tp", None),
            P(None, "fsdp", "tp", None),
            P(None, "fsdp", "tp", None),
            P("fsdp", "tp", None),
            P(None, ("fsdp", "tp")),
            P(None, ("fsdp", "tp")),
            P(None, ("fsdp", "tp")),
        ),
        check_vma=False,
    )
```

profile of v0, /device:TPU:0, one launch (start us, length us, event | category | flops | bytes accessed | tf_op | source)
XLA Modules:
  0.0 411.3 jit_solution(16580479824753953919)
XLA Ops:
  8.0 1.1 fusion.25
  9.1 1.5 fusion.24
  11.0 2.3 broadcast_in_dim.46
  13.3 16.8 %while.4 = (s32[]{:T(128)}, bf16[16,56,2432]{2,1,0:T(8,128)(2,1)}, s32[2,2]{1,0:T(2,128)S(1)}, bf16[2,56,448]{2,1,0:T(8,128)(2,1)S(1)}, s32[]{:T(128)}, /*index=5*/s32[3]{0:T(128)S(1)}, s32[1]{0:T(128)}, s32[]{:T(128)}) while((s32[]{:T(128)}, bf16[16,56,2432]{2,1,0:T(8,128)(2,1)}, s32[2,2]{1,0:T(2,128)S(1)}, bf16[2,56,448]{2,1,0:T(8,128)(2,1)S(1)}, ...), condition=%wide.while_cond, body=%wide.while_body.sunk | while | flops 25107 | bytes 251051 | solution.py:61
  13.9 2.0 and_reduce_fusion.8
  15.9 2.9 dynamic-slice_select_fusion.8
  18.8 2.9 dynamic-update-slice.12
  22.3 2.0 and_reduce_fusion.8
  24.3 2.9 dynamic-slice_select_fusion.8
  27.2 2.9 dynamic-update-slice.12
  30.1 16.1 %while.5 = (s32[]{:T(128)}, bf16[16,56,2432]{2,1,0:T(8,128)(2,1)}, s32[2,2]{1,0:T(2,128)S(1)}, bf16[2,56,64]{2,1,0:T(8,128)(2,1)S(1)}, s32[]{:T(128)}, /*index=5*/s32[3]{0:T(128)S(1)}, s32[1]{0:T(128)}, s32[]{:T(128)}) while((s32[]{:T(128)}, bf16[16,56,2432]{2,1,0:T(8,128)(2,1)}, s32[2,2]{1,0:T(2,128)S(1)}, bf16[2,56,64]{2,1,0:T(8,128)(2,1)S(1)}, ...), condition=%wide.while_cond.1, body=%wide.while_body.1.sunk | while | flops 3603 | bytes 36011 | solution.py:61
  30.7 2.0 and_reduce_fusion.9
  32.7 2.8 dynamic-slice_select_fusion.9
  35.5 2.7 dynamic-update-slice.13
  38.7 2.0 and_reduce_fusion.9
  40.7 2.8 dynamic-slice_select_fusion.9
  43.5 2.7 dynamic-update-slice.13
  46.2 16.1 %while.6 = (s32[]{:T(128)}, bf16[16,56,2432]{2,1,0:T(8,128)(2,1)}, s32[2,2]{1,0:T(2,128)S(1)}, bf16[2,56,64]{2,1,0:T(8,128)(2,1)S(1)}, s32[]{:T(128)}, /*index=5*/s32[3]{0:T(128)S(1)}, s32[1]{0:T(128)}, s32[]{:T(128)}) while((s32[]{:T(128)}, bf16[16,56,2432]{2,1,0:T(8,128)(2,1)}, s32[2,2]{1,0:T(2,128)S(1)}, bf16[2,56,64]{2,1,0:T(8,128)(2,1)S(1)}, ...), condition=%wide.while_cond.2, body=%wide.while_body.2.sunk | while | flops 3603 | bytes 36011 | solution.py:61
  46.8 2.0 and_reduce_fusion.10
  48.8 2.8 dynamic-slice_select_fusion.10
  51.5 2.7 dynamic-update-slice.14
  54.8 2.0 and_reduce_fusion.10
  56.8 2.8 dynamic-slice_select_fusion.10
  59.6 2.7 dynamic-update-slice.14
  62.3 16.7 %while.7 = (s32[]{:T(128)}, bf16[16,56,2432]{2,1,0:T(8,128)(2,1)}, s32[2,2]{1,0:T(2,128)S(1)}, bf16[2,56,448]{2,1,0:T(8,128)(2,1)S(1)}, s32[]{:T(128)}, /*index=5*/s32[3]{0:T(128)S(1)}, s32[1]{0:T(128)}, s32[]{:T(128)}) while((s32[]{:T(128)}, bf16[16,56,2432]{2,1,0:T(8,128)(2,1)}, s32[2,2]{1,0:T(2,128)S(1)}, bf16[2,56,448]{2,1,0:T(8,128)(2,1)S(1)}, ...), condition=%wide.while_cond.3, body=%wide.while_body.3.sunk | while | flops 25107 | bytes 251051 | solution.py:61
  62.9 2.0 and_reduce_fusion.11
  64.9 2.9 dynamic-slice_select_fusion.11
  67.8 2.9 dynamic-update-slice.15
  71.2 2.0 and_reduce_fusion.11
  73.2 2.9 dynamic-slice_select_fusion.11
  76.2 2.9 dynamic-update-slice.15
  79.0 2.4 scatter_fusion
  81.5 2.4 scatter_fusion.1
  83.9 2.4 scatter_fusion.2
  86.3 8.5 %all-to-all-start = ((bf16[16,56,2432]{2,1,0:T(8,128)(2,1)}), bf16[16,56,2432]{2,1,0:T(8,128)(2,1)}, u32[]{:S(2)}, u32[]{:S(2)}) async-start(bf16[16,56,2432]{2,1,0:T(8,128)(2,1)} %scatter_fusion.2), calls=%async_computation | async-start | bytes 8716288 | tf_op jit(solution)/shard_map/all_to_all | solution.py:64
  98.0 10.3 %all-gather.3.cloned.1.call-done = bf16[1,896,896]{2,1,0:T(8,128)(2,1)} async-done(((bf16[1,448,896]{2,1,0:T(8,128)(2,1)}), bf16[1,896,896]{2,1,0:T(8,128)(2,1)}) %all-gather.3.cloned.1.call-update) | async-done | bytes 1605648 | tf_op jit(solution)/shard_map/all_gather | solution.py:99
  108.3 69.2 %all-to-all-done = bf16[16,56,2432]{2,1,0:T(8,128)(2,1)} async-done(((bf16[16,56,2432]{2,1,0:T(8,128)(2,1)}), bf16[16,56,2432]{2,1,0:T(8,128)(2,1)}, u32[]{:S(2)}, u32[]{:S(2)}) %all-to-all-start) | async-done | bytes 4358176 | tf_op jit(solution)/shard_map/all_to_all | solution.py:64
  177.5 5.1 %conditional.2 = (bf16[896,2432]{0,1:T(8,128)(2,1)}) conditional(s32[]{:T(128)} %clamp.4, (bf16[896,2432]{1,0:T(8,128)(2,1)}, bf16[896,896]{1,0:T(8,128)(2,1)}) %tuple.144, (bf16[896,2432]{1,0:T(8,128)(2,1)}, bf16[896,896]{1,0:T(8,128)(2,1)}) %tuple.145, (bf16[896,896]{1,0:T(8,128)(2,1)}, bf16[896,2432]{1,0:T(8,128)(2,1)}) %tuple.146), branch_computations={%region_9.0_spmd, %region_10.0_spmd, %region_11.0_spmd} | conditional | flops 3904897024 | bytes 10321928 | solution.py:97
  177.5 2.8 fusion
  180.3 2.3 pad.10
  182.7 7.1 %copy.72 = bf16[896,2432]{1,0:T(8,128)(2,1)} copy(bf16[896,2432]{0,1:T(8,128)(2,1)} %get-tuple-element.397) | data formatting | bytes 8716288 | tf_op jit(solution)/shard_map/cond | solution.py:97
  189.8 25.4 %all-to-all-start.1 = ((bf16[16,56,2432]{2,1,0:T(8,128)(2,1)}), bf16[16,56,2432]{2,1,0:T(8,128)(2,1)}, u32[]{:S(2)}, u32[]{:S(2)}) async-start(bf16[16,56,2432]{2,1,0:T(8,128)(2,1)} %bitcast.96), calls=%async_computation.1 | async-start | bytes 8716288 | tf_op jit(solution)/shard_map/all_to_all | solution.py:101
  215.2 4.5 %conditional.3 = (f32[896,896]{1,0:T(8,128)}) conditional(s32[]{:T(128)} %clamp.4, bf16[896,2432]{1,0:T(8,128)(2,1)} %bitcast.1, bf16[896,2432]{1,0:T(8,128)(2,1)} %bitcast.1, bf16[896,2432]{1,0:T(8,128)(2,1)} %bitcast.1), branch_computations={%region_28.29_spmd, %region_29.30_spmd, %region_30.31_spmd} | conditional | flops 3904897024 | bytes 7569416 | solution.py:83
  215.4 4.4 %fusion.4 = f32[896,896]{1,0:T(8,128)} fusion(bf16[896,2432]{1,0:T(8,128)(2,1)} %param.3), kind=kOutput, calls=%fused_computation.14 | convolution fusion | flops 719323136 | bytes 4128768 | tf_op jit(solution)/shard_map/cond/branch_0_fun/dot_general | solution.py:35
  219.8 1.5 copy-done.1
  221.3 20.8 %divide_multiply_fusion = (f32[2,56,1,8320]{3,2,1,0:T(1,128)S(1)}, f32[2,56,1,8320]{3,2,1,0:T(1,128)}, f32[2,56,1,8320]{3,2,1,0:T(1,128)}) fusion(bf16[2,56,1,8320]{3,1,2,0:T(8,128)(2,1)S(1)} %copy-done.1, f32[2,56,1,8320]{3,2,1,0:T(1,128)} %param.22, f32[2,56,1,8320]{3,2,1,0:T(1,128)} %param.21), kind=kLoop, calls=%fused_computation.36 | loop fusion | flops 10250240 | bytes 20500480 | tf_op jit(solution)/shard_map/mul | solution.py:57
  242.5 1.8 copy-done
  244.7 1.2 slice_reduce_fusion.8
  246.1 2.2 slice_reduce_fusion.3
  249.4 3.4 fusion.10
  252.7 43.8 %all-to-all-done.1 = bf16[16,56,2432]{2,1,0:T(8,128)(2,1)} async-done(((bf16[16,56,2432]{2,1,0:T(8,128)(2,1)}), bf16[16,56,2432]{2,1,0:T(8,128)(2,1)}, u32[]{:S(2)}, u32[]{:S(2)}) %all-to-all-start.1) | async-done | bytes 4358176 | tf_op jit(solution)/shard_map/all_to_all | solution.py:101
  296.5 12.8 %copy.73 = bf16[16,56,2432]{1,0,2:T(8,128)(2,1)} copy(bf16[16,56,2432]{2,1,0:T(8,128)(2,1)} %all-to-all-done.1) | data formatting | bytes 8716288 | tf_op jit(solution)/shard_map/all_to_all | solution.py:101
  309.3 1.8 gather_fusion.2
  311.8 1.8 gather_fusion.1
  314.3 3.1 gather_fusion.3
  317.4 2.9 gather_fusion
  321.9 2.9 gather_fusion.4
  324.7 2.9 gather_fusion.5
  327.6 2.9 gather_fusion.6
  330.5 2.8 concatenate.57
  337.4 55.1 %all-reduce.6 = (f32[2,7]{1,0:T(2,128)S(1)}, f32[2,7]{1,0:T(2,128)S(1)}) all-reduce(f32[2,7]{1,0:T(2,128)S(1)} %stack.63, f32[2,7]{1,0:T(2,128)S(1)} %stack.55), channel_id=1, replica_groups=mesh['fsdp'=16,'tp'=2] {'fsdp','tp'}, use_global_device_ids=true, to_apply=%region_27.28 | all-reduce | flops 28 | bytes 224 | tf_op jit(solution)/shard_map/psum | solution.py:107
  392.8 2.8 concatenate.56
  396.2 2.6 copy_subtract_fusion
  398.8 5.7 %copy.101 = f32[2,56,1,8320]{3,2,1,0:T(1,128)} copy(f32[2,56,1,8320]{3,1,0,2:T(8,128)S(1)} %copy_subtract_fusion) | data formatting | bytes 7454720
  (104 shorter events, 17.7 us)
Async XLA Ops:
  7.2 3.5 copy-start.9
  9.1 4.2 %copy-start.10 = (s32[3]{0:T(128)S(1)}, s32[3]{0:T(128)}, u32[]{:S(2)}) copy-start(s32[3]{0:T(128)} %constant.291) | copy-start | bytes 40
  10.6 19.5 %copy-start.11 = (s32[3]{0:T(128)S(1)}, s32[3]{0:T(128)}, u32[]{:S(2)}) copy-start(s32[3]{0:T(128)} %constant.305) | copy-start | bytes 40
  86.3 9.9 %copy-start.15 = (s32[7]{0:T(128)S(1)}, s32[7]{0:T(128)}, u32[]{:S(2)}) copy-start(s32[7]{0:T(128)} %constant.14.clone) | copy-start | bytes 88
  86.3 91.2 %all-to-all-start = ((bf16[16,56,2432]{2,1,0:T(8,128)(2,1)}), bf16[16,56,2432]{2,1,0:T(8,128)(2,1)}, u32[]{:S(2)}, u32[]{:S(2)}) async-start(bf16[16,56,2432]{2,1,0:T(8,128)(2,1)} %scatter_fusion.2), calls=%async_computation | async-start | bytes 8716288 | tf_op jit(solution)/shard_map/all_to_all | solution.py:64
  94.8 13.5 %all-gather.3.cloned.1.call-start = ((), (), s32[]{:S(2)}) async-start(), calls=%async_computation.4 | async-start | bytes 2408448 | tf_op jit(solution)/shard_map/all_gather | solution.py:99
  189.8 106.8 %all-to-all-start.1 = ((bf16[16,56,2432]{2,1,0:T(8,128)(2,1)}), bf16[16,56,2432]{2,1,0:T(8,128)(2,1)}, u32[]{:S(2)}, u32[]{:S(2)}) async-start(bf16[16,56,2432]{2,1,0:T(8,128)(2,1)} %bitcast.96), calls=%async_computation.1 | async-start | bytes 8716288 | tf_op jit(solution)/shard_map/all_to_all | solution.py:101
  215.2 34.2 %reduce-scatter.2.cloned.1.call-start = ((), (), s32[]{:S(2)}) async-start(), calls=%async_computation.3 | async-start | bytes 4816896 | tf_op jit(solution)/shard_map/reduce_scatter | solution.py:85
  219.8 1.5 copy-start.1
  242.4 1.9 copy-start
  242.4 6.3 %copy-start.12 = (f32[2,92]{1,0:T(2,128)S(1)}, f32[2,92]{1,0:T(2,128)}, u32[]{:S(2)}) copy-start(f32[2,92]{1,0:T(2,128)} %param.25) | copy-start | bytes 2212
  242.4 6.3 %copy-start.13 = (f32[2,92]{1,0:T(2,128)S(1)}, f32[2,92]{1,0:T(2,128)}, u32[]{:S(2)}) copy-start(f32[2,92]{1,0:T(2,128)} %param.27) | copy-start | bytes 2212
  242.4 6.3 %copy-start.14 = (f32[2,92]{1,0:T(2,128)S(1)}, f32[2,92]{1,0:T(2,128)}, u32[]{:S(2)}) copy-start(f32[2,92]{1,0:T(2,128)} %param.28) | copy-start | bytes 2212
  242.4 6.3 %copy-start.16 = (bf16[2,92]{1,0:T(2,128)(2,1)S(1)}, bf16[2,92]{1,0:T(2,128)(2,1)}, u32[]{:S(2)}) copy-start(bf16[2,92]{1,0:T(2,128)(2,1)} %param.26) | copy-start | bytes 1108
  242.5 6.9 %copy-start.2 = (f32[1,448,896]{2,1,0:T(8,128)S(1)}, f32[1,448,896]{2,1,0:T(8,128)}, u32[]{:S(2)}) copy-start(f32[1,448,896]{2,1,0:T(8,128)} %param.23) | copy-start | bytes 4816900
  313.6 3.8 copy-start.7
  317.4 10.2 %copy-start.5 = (bf16[2,56,448]{1,0,2:T(2,128)(2,1)}, bf16[2,56,448]{1,0,2:T(2,128)(2,1)S(1)}, u32[]{:S(2)}) copy-start(bf16[2,56,448]{1,0,2:T(2,128)(2,1)S(1)} %gather_fusion.3) | copy-start | bytes 301060
  320.3 7.3 %copy-start.3 = (bf16[2,56,448]{1,0,2:T(2,128)(2,1)}, bf16[2,56,448]{1,0,2:T(2,128)(2,1)S(1)}, u32[]{:S(2)}) copy-start(bf16[2,56,448]{1,0,2:T(2,128)(2,1)S(1)} %gather_fusion) | copy-start | bytes 301060
  333.6 1.5 copy-start.8
  333.6 1.6 copy-start.6
  333.6 3.1 copy-start.4
Sparse Core Ops, SparseCore 0:
  97.2 11.0 all-gather.2
  219.9 17.0 reduce-scatter.1
where the time goes:
time: 415 us; the launch traced here: 411 us
  waiting for transfers between devices  124 us (30%)
  local copies, waits for them, and re-layouts  103 us (25%)
  other arithmetic  72.3 us (17%)
  blocking collectives  55.1 us (13%)
  starting transfers between devices  34 us (8%)
  between operations  15.6 us (4%)
  matrix products  7.14 us (2%)
    all_to_all x1, waiting for transfers between devices, on_device(): lax.all_to_all(outgoing, 'fsdp', split_axis=0, concat_axis=0, tiled=True)  69.2 us
    psum x1, blocking collectives, on_device(): shampoo_total = lax.psum(shampoo_part, ('fsdp', 'tp'))  55.1 us
    all_to_all x1, waiting for transfers between devices, on_device(): lax.all_to_all(precond.reshape(chips, rows, capacity), 'fsdp', split_axis...  43.8 us
    scatter x16, other arithmetic  38.8 us
    scatter x24, local copies, waits for them, and re-layouts  26.9 us
    all_to_all x1, starting transfers between devices, on_device(): lax.all_to_all(precond.reshape(chips, rows, capacity), 'fsdp', split_axis...  25.4 us
    gather x11, local copies, waits for them, and re-layouts, on_device(): pieces = [returned[owner[:, kind], :, :widths[kind]] for kind in range(7)]  21.1 us
    mul x1, other arithmetic, on_device(): adam_part = kind_sums(adam_step * adam_step, widths, starts)  20.8 us
  transfers between devices with their start and end apart: 4, of which 3 were waited for; matrix products, arithmetic and copies ran while one was open for 9% of the time, Pallas kernels for 0%

commit v1 on v0

--- a/solution.py
+++ b/solution.py
@@ -104,7 +104,7 @@
     pieces = [returned[owner[:, kind], :, : widths[kind]] for kind in range(7)]
     direction = jnp.concatenate(pieces, axis=2).astype(jnp.float32)
     shampoo_part = kind_sums(direction * direction, widths, starts)
-    shampoo_total = lax.psum(shampoo_part, ("fsdp", "tp"))
+    shampoo_total = jnp.sum(lax.all_gather(shampoo_part, ("fsdp", "tp")), axis=0)
     ratio = jnp.sqrt(adam_total) / (jnp.sqrt(shampoo_total) + 1e-06)
     column_scale = jnp.concatenate(
         [jnp.broadcast_to(ratio[:, kind : kind + 1], (layers, widths[kind])) for kind in range(7)],

time: 415 us -> 440 us (1.060)
  blocking collectives: 55.1 us -> 124 us
  waiting for transfers between devices: 124 us -> 80.2 us
    all_to_all x1, waiting for transfers between devices: 43.8 us -> 0.01 us  [on_device(): lax.all_to_all(precond.reshape(chips, rows, capacity), 'fsdp', split_axis...]
    all_gather x0 -> x1, blocking collectives: none -> 41.1 us  [on_device(): lax.all_gather(shampoo_part, ('fsdp', 'tp'))]
    psum x1, blocking collectives: 55.1 us -> 82.8 us  [on_device(): adam_total = lax.psum(adam_part, ('fsdp', 'tp'))]
  transfers between devices with their start and end apart: 4 -> 4, of which waited for: 3 -> 2; matrix products, arithmetic and copies ran while one was open for 9% -> 8% of each run, Pallas kernels for 0% -> 0%
where the time goes in v1:
time: 440 us; the launch traced here: 436 us
  blocking collectives  124 us (28%)
  local copies, waits for them, and re-layouts  103 us (23%)
  waiting for transfers between devices  80.2 us (18%)
  other arithmetic  72.4 us (16%)
  starting transfers between devices  34 us (8%)
  between operations  15.6 us (4%)
  matrix products  7.14 us (2%)
    psum x1, blocking collectives, on_device(): adam_total = lax.psum(adam_part, ('fsdp', 'tp'))  82.8 us
    all_to_all x1, waiting for transfers between devices, on_device(): lax.all_to_all(outgoing, 'fsdp', split_axis=0, concat_axis=0, tiled=True)  69.2 us
    all_gather x1, blocking collectives, on_device(): lax.all_gather(shampoo_part, ('fsdp', 'tp'))  41.1 us
    scatter x16, other arithmetic  38.8 us
    scatter x24, local copies, waits for them, and re-layouts  26.9 us
    all_to_all x1, starting transfers between devices, on_device(): lax.all_to_all(precond.reshape(chips, rows, capacity), 'fsdp', split_axis...  25.4 us
    gather x11, local copies, waits for them, and re-layouts, on_device(): pieces = [returned[owner[:, kind], :, :widths[kind]] for kind in range(7)]  21.1 us
    mul x1, other arithmetic, on_device(): adam_part = kind_sums(adam_step * adam_step, widths, starts)  20.8 us
  transfers between devices with their start and end apart: 4, of which 2 were waited for; matrix products, arithmetic and copies ran while one was open for 8% of the time, Pallas kernels for 0%

profile of v1, /device:TPU:0, one launch (start us, length us, event | category | flops | bytes accessed | tf_op | source)
XLA Modules:
  0.0 436.4 jit_solution(182656982739101708)
XLA Ops:
  8.0 1.1 fusion.25
  9.1 1.5 fusion.24
  11.0 2.3 broadcast_in_dim.46
  13.3 16.8 %while.4 = (s32[]{:T(128)}, bf16[16,56,2432]{2,1,0:T(8,128)(2,1)}, s32[2,2]{1,0:T(2,128)S(1)}, bf16[2,56,448]{2,1,0:T(8,128)(2,1)S(1)}, s32[]{:T(128)}, /*index=5*/s32[3]{0:T(128)S(1)}, s32[1]{0:T(128)}, s32[]{:T(128)}) while((s32[]{:T(128)}, bf16[16,56,2432]{2,1,0:T(8,128)(2,1)}, s32[2,2]{1,0:T(2,128)S(1)}, bf16[2,56,448]{2,1,0:T(8,128)(2,1)S(1)}, ...), condition=%wide.while_cond, body=%wide.while_body.sunk | while | flops 25107 | bytes 251051 | solution.py:61
  13.9 2.0 and_reduce_fusion.8
  15.9 2.9 dynamic-slice_select_fusion.8
  18.8 2.9 dynamic-update-slice.12
  22.3 2.0 and_reduce_fusion.8
  24.3 2.9 dynamic-slice_select_fusion.8
  27.2 2.9 dynamic-update-slice.12
  30.1 16.1 %while.5 = (s32[]{:T(128)}, bf16[16,56,2432]{2,1,0:T(8,128)(2,1)}, s32[2,2]{1,0:T(2,128)S(1)}, bf16[2,56,64]{2,1,0:T(8,128)(2,1)S(1)}, s32[]{:T(128)}, /*index=5*/s32[3]{0:T(128)S(1)}, s32[1]{0:T(128)}, s32[]{:T(128)}) while((s32[]{:T(128)}, bf16[16,56,2432]{2,1,0:T(8,128)(2,1)}, s32[2,2]{1,0:T(2,128)S(1)}, bf16[2,56,64]{2,1,0:T(8,128)(2,1)S(1)}, ...), condition=%wide.while_cond.1, body=%wide.while_body.1.sunk | while | flops 3603 | bytes 36011 | solution.py:61
  30.7 2.0 and_reduce_fusion.9
  32.7 2.8 dynamic-slice_select_fusion.9
  35.5 2.7 dynamic-update-slice.13
  38.7 2.0 and_reduce_fusion.9
  40.7 2.8 dynamic-slice_select_fusion.9
  43.5 2.7 dynamic-update-slice.13
  46.2 16.1 %while.6 = (s32[]{:T(128)}, bf16[16,56,2432]{2,1,0:T(8,128)(2,1)}, s32[2,2]{1,0:T(2,128)S(1)}, bf16[2,56,64]{2,1,0:T(8,128)(2,1)S(1)}, s32[]{:T(128)}, /*index=5*/s32[3]{0:T(128)S(1)}, s32[1]{0:T(128)}, s32[]{:T(128)}) while((s32[]{:T(128)}, bf16[16,56,2432]{2,1,0:T(8,128)(2,1)}, s32[2,2]{1,0:T(2,128)S(1)}, bf16[2,56,64]{2,1,0:T(8,128)(2,1)S(1)}, ...), condition=%wide.while_cond.2, body=%wide.while_body.2.sunk | while | flops 3603 | bytes 36011 | solution.py:61
  46.8 2.0 and_reduce_fusion.10
  48.8 2.8 dynamic-slice_select_fusion.10
  51.5 2.7 dynamic-update-slice.14
  54.8 2.0 and_reduce_fusion.10
  56.8 2.8 dynamic-slice_select_fusion.10
  59.6 2.7 dynamic-update-slice.14
  62.3 16.7 %while.7 = (s32[]{:T(128)}, bf16[16,56,2432]{2,1,0:T(8,128)(2,1)}, s32[2,2]{1,0:T(2,128)S(1)}, bf16[2,56,448]{2,1,0:T(8,128)(2,1)S(1)}, s32[]{:T(128)}, /*index=5*/s32[3]{0:T(128)S(1)}, s32[1]{0:T(128)}, s32[]{:T(128)}) while((s32[]{:T(128)}, bf16[16,56,2432]{2,1,0:T(8,128)(2,1)}, s32[2,2]{1,0:T(2,128)S(1)}, bf16[2,56,448]{2,1,0:T(8,128)(2,1)S(1)}, ...), condition=%wide.while_cond.3, body=%wide.while_body.3.sunk | while | flops 25107 | bytes 251051 | solution.py:61
  62.9 2.0 and_reduce_fusion.11
  64.9 2.9 dynamic-slice_select_fusion.11
  67.8 2.9 dynamic-update-slice.15
  71.2 2.0 and_reduce_fusion.11
  73.2 2.9 dynamic-slice_select_fusion.11
  76.2 2.9 dynamic-update-slice.15
  79.0 2.4 scatter_fusion
  81.5 2.4 scatter_fusion.1
  83.9 2.4 scatter_fusion.2
  86.3 8.5 %all-to-all-start = ((bf16[16,56,2432]{2,1,0:T(8,128)(2,1)}), bf16[16,56,2432]{2,1,0:T(8,128)(2,1)}, u32[]{:S(2)}, u32[]{:S(2)}) async-start(bf16[16,56,2432]{2,1,0:T(8,128)(2,1)} %scatter_fusion.2), calls=%async_computation | async-start | bytes 8716288 | tf_op jit(solution)/shard_map/all_to_all | solution.py:64
  98.0 10.3 %all-gather.5.cloned.1.call-done = bf16[1,896,896]{2,1,0:T(8,128)(2,1)} async-done(((bf16[1,448,896]{2,1,0:T(8,128)(2,1)}), bf16[1,896,896]{2,1,0:T(8,128)(2,1)}) %all-gather.5.cloned.1.call-update) | async-done | bytes 1605648 | tf_op jit(solution)/shard_map/all_gather | solution.py:99
  108.3 69.2 %all-to-all-done = bf16[16,56,2432]{2,1,0:T(8,128)(2,1)} async-done(((bf16[16,56,2432]{2,1,0:T(8,128)(2,1)}), bf16[16,56,2432]{2,1,0:T(8,128)(2,1)}, u32[]{:S(2)}, u32[]{:S(2)}) %all-to-all-start) | async-done | bytes 4358176 | tf_op jit(solution)/shard_map/all_to_all | solution.py:64
  177.5 5.1 %conditional.2 = (bf16[896,2432]{0,1:T(8,128)(2,1)}) conditional(s32[]{:T(128)} %clamp.4, (bf16[896,2432]{1,0:T(8,128)(2,1)}, bf16[896,896]{1,0:T(8,128)(2,1)}) %tuple.144, (bf16[896,2432]{1,0:T(8,128)(2,1)}, bf16[896,896]{1,0:T(8,128)(2,1)}) %tuple.145, (bf16[896,896]{1,0:T(8,128)(2,1)}, bf16[896,2432]{1,0:T(8,128)(2,1)}) %tuple.146), branch_computations={%region_9.0_spmd, %region_10.0_spmd, %region_11.0_spmd} | conditional | flops 3904897024 | bytes 10321928 | solution.py:97
  177.5 2.8 fusion
  180.3 2.3 pad.10
  182.7 7.1 %copy.74 = bf16[896,2432]{1,0:T(8,128)(2,1)} copy(bf16[896,2432]{0,1:T(8,128)(2,1)} %get-tuple-element.395) | data formatting | bytes 8716288 | tf_op jit(solution)/shard_map/cond | solution.py:97
  189.8 25.4 %all-to-all-start.1 = ((bf16[16,56,2432]{2,1,0:T(8,128)(2,1)}), bf16[16,56,2432]{2,1,0:T(8,128)(2,1)}, u32[]{:S(2)}, u32[]{:S(2)}) async-start(bf16[16,56,2432]{2,1,0:T(8,128)(2,1)} %bitcast.97), calls=%async_computation.1 | async-start | bytes 8716288 | tf_op jit(solution)/shard_map/all_to_all | solution.py:101
  215.2 4.5 %conditional.3 = (f32[896,896]{1,0:T(8,128)}) conditional(s32[]{:T(128)} %clamp.4, bf16[896,2432]{1,0:T(8,128)(2,1)} %bitcast.1, bf16[896,2432]{1,0:T(8,128)(2,1)} %bitcast.1, bf16[896,2432]{1,0:T(8,128)(2,1)} %bitcast.1), branch_computations={%region_28.29_spmd, %region_29.30_spmd, %region_30.31_spmd} | conditional | flops 3904897024 | bytes 7569416 | solution.py:83
  215.4 4.4 fusion.4
  219.8 1.5 copy-done.1
  221.3 20.8 %divide_multiply_fusion = (f32[2,56,1,8320]{3,2,1,0:T(1,128)S(1)}, f32[2,56,1,8320]{3,2,1,0:T(1,128)}, f32[2,56,1,8320]{3,2,1,0:T(1,128)}) fusion(bf16[2,56,1,8320]{3,1,2,0:T(8,128)(2,1)S(1)} %copy-done.1, f32[2,56,1,8320]{3,2,1,0:T(1,128)} %param.22, f32[2,56,1,8320]{3,2,1,0:T(1,128)} %param.21), kind=kLoop, calls=%fused_computation.36 | loop fusion | flops 10250240 | bytes 20500480 | tf_op jit(solution)/shard_map/mul | solution.py:57
  242.5 1.8 copy-done
  244.7 1.2 slice_reduce_fusion.8
  246.1 2.2 slice_reduce_fusion.3
  248.7 82.8 %psum.7 = f32[2,7]{1,0:T(2,128)S(1)} all-reduce(f32[2,7]{1,0:T(2,128)S(1)} %stack.55), channel_id=1, replica_groups=mesh['fsdp'=16,'tp'=2] {'fsdp','tp'}, use_global_device_ids=true, to_apply=%region_19.20 | all-reduce | flops 14 | bytes 112 | tf_op jit(solution)/shard_map/psum | solution.py:58
  332.2 3.4 fusion.10
  335.6 12.8 %copy.75 = bf16[16,56,2432]{1,0,2:T(8,128)(2,1)} copy(bf16[16,56,2432]{2,1,0:T(8,128)(2,1)} %all-to-all-done.1) | data formatting | bytes 8716288 | tf_op jit(solution)/shard_map/all_to_all | solution.py:101
  348.4 1.8 gather_fusion.2
  350.8 1.8 gather_fusion.1
  353.3 3.1 gather_fusion.3
  356.4 2.9 gather_fusion
  360.9 2.9 gather_fusion.4
  363.7 2.9 gather_fusion.5
  366.6 2.9 gather_fusion.6
  369.5 2.8 concatenate.57
  376.5 41.1 %all-gather.2 = f32[32,2,7]{2,1,0:T(2,128)S(1)} all-gather(f32[1,2,7]{2,1,0:T(2,128)S(1)} %bitcast.114), channel_id=3, replica_groups=mesh['fsdp'=16,'tp'=2] {'fsdp','tp'}, dimensions={0}, use_global_device_ids=true | all-gather | bytes 1848 | tf_op jit(solution)/shard_map/all_gather | solution.py:107
  417.9 2.8 concatenate.56
  421.4 2.6 copy_subtract_fusion
  423.9 5.7 %copy.103 = f32[2,56,1,8320]{3,2,1,0:T(1,128)} copy(f32[2,56,1,8320]{3,1,0,2:T(8,128)S(1)} %copy_subtract_fusion) | data formatting | bytes 7454720
  (106 shorter events, 17.8 us)
Async XLA Ops:
  7.2 3.5 copy-start.9
  9.1 4.2 copy-start.10
  10.6 19.5 %copy-start.11 = (s32[3]{0:T(128)S(1)}, s32[3]{0:T(128)}, u32[]{:S(2)}) copy-start(s32[3]{0:T(128)} %constant.305) | copy-start | bytes 40
  86.3 9.9 %copy-start.15 = (s32[7]{0:T(128)S(1)}, s32[7]{0:T(128)}, u32[]{:S(2)}) copy-start(s32[7]{0:T(128)} %constant.14.clone) | copy-start | bytes 88
  86.3 91.2 %all-to-all-start = ((bf16[16,56,2432]{2,1,0:T(8,128)(2,1)}), bf16[16,56,2432]{2,1,0:T(8,128)(2,1)}, u32[]{:S(2)}, u32[]{:S(2)}) async-start(bf16[16,56,2432]{2,1,0:T(8,128)(2,1)} %scatter_fusion.2), calls=%async_computation | async-start | bytes 8716288 | tf_op jit(solution)/shard_map/all_to_all | solution.py:64
  94.8 13.5 %all-gather.5.cloned.1.call-start = ((), (), s32[]{:S(2)}) async-start(), calls=%async_computation.4 | async-start | bytes 2408448 | tf_op jit(solution)/shard_map/all_gather | solution.py:99
  189.8 145.8 %all-to-all-start.1 = ((bf16[16,56,2432]{2,1,0:T(8,128)(2,1)}), bf16[16,56,2432]{2,1,0:T(8,128)(2,1)}, u32[]{:S(2)}, u32[]{:S(2)}) async-start(bf16[16,56,2432]{2,1,0:T(8,128)(2,1)} %bitcast.97), calls=%async_computation.1 | async-start | bytes 8716288 | tf_op jit(solution)/shard_map/all_to_all | solution.py:101
  215.2 117.0 %reduce-scatter.2.cloned.1.call-start = ((), (), s32[]{:S(2)}) async-start(), calls=%async_computation.3 | async-start | bytes 4816896 | tf_op jit(solution)/shard_map/reduce_scatter | solution.py:85
  219.8 1.5 copy-start.1
  242.4 1.9 copy-start
  242.4 89.2 %copy-start.12 = (f32[2,92]{1,0:T(2,128)S(1)}, f32[2,92]{1,0:T(2,128)}, u32[]{:S(2)}) copy-start(f32[2,92]{1,0:T(2,128)} %param.25) | copy-start | bytes 2212
  242.4 89.2 %copy-start.13 = (f32[2,92]{1,0:T(2,128)S(1)}, f32[2,92]{1,0:T(2,128)}, u32[]{:S(2)}) copy-start(f32[2,92]{1,0:T(2,128)} %param.27) | copy-start | bytes 2212
  242.4 89.2 %copy-start.14 = (f32[2,92]{1,0:T(2,128)S(1)}, f32[2,92]{1,0:T(2,128)}, u32[]{:S(2)}) copy-start(f32[2,92]{1,0:T(2,128)} %param.28) | copy-start | bytes 2212
  242.4 89.2 %copy-start.16 = (bf16[2,92]{1,0:T(2,128)(2,1)S(1)}, bf16[2,92]{1,0:T(2,128)(2,1)}, u32[]{:S(2)}) copy-start(bf16[2,92]{1,0:T(2,128)(2,1)} %param.26) | copy-start | bytes 1108
  242.5 89.7 %copy-start.2 = (f32[1,448,896]{2,1,0:T(8,128)S(1)}, f32[1,448,896]{2,1,0:T(8,128)}, u32[]{:S(2)}) copy-start(f32[1,448,896]{2,1,0:T(8,128)} %param.23) | copy-start | bytes 4816900
  352.6 0.7 copy-start.7
  356.4 10.2 %copy-start.3 = (bf16[2,56,448]{1,0,2:T(2,128)(2,1)}, bf16[2,56,448]{1,0,2:T(2,128)(2,1)S(1)}, u32[]{:S(2)}) copy-start(bf16[2,56,448]{1,0,2:T(2,128)(2,1)S(1)} %gather_fusion.3) | copy-start | bytes 301060
  359.3 7.3 %copy-start.5 = (bf16[2,56,448]{1,0,2:T(2,128)(2,1)}, bf16[2,56,448]{1,0,2:T(2,128)(2,1)S(1)}, u32[]{:S(2)}) copy-start(bf16[2,56,448]{1,0,2:T(2,128)(2,1)S(1)} %gather_fusion) | copy-start | bytes 301060
  372.6 1.5 copy-start.8
  372.6 1.6 copy-start.4
  372.6 2.3 copy-start.6
Sparse Core Ops, SparseCore 0:
  97.2 11.0 all-gather.4
  219.9 17.0 reduce-scatter.1
